TPU v7x, 256 devices: a whole 4x4x8 slice. The times are simulated.
256 devices in a mesh: dom: 16 (over y, z_lo, core), dir: 16 (over x, z_hi).
Axes of the slice: x: 4, y: 4, z: 8 (z_hi: 4, z_lo: 2; z = z_hi * 2 + z_lo), core: 2. Of those that a mesh axis runs over, the one named last changes fastest.
Arguments:
- coefficients: bfloat16 [2, 70, 32768], P(None, None, ('dom', 'dir')), may hold values from -6 to 6
- positions: float32 [3, 32768], P(None, ('dom', 'dir')), may hold values from -50 to 50
- polar: float32 [10240], P('dir'), may hold values from 0 to 1.4
- azimuth: float32 [10240], P('dir'), may hold values from -3.140625 to 3.140625
- weights: float32 [10240], P('dir'), may hold values from -4 to 4
- farmap: float32 [2, 2, 70, 10240], P(None, None, None, 'dir'), may hold values from -0.00390625 to 0.00390625
Outputs:
- coef_grad: float32 [2, 70, 32768], P(None, None, ('dom', 'dir'))
- place_grad: float32 [3, 32768], P(None, ('dom', 'dir'))
All inputs are finite; a program needn't handle non-finite values.
Results may differ from a plain program's by a relative error of at most 0.0052.
Values may be sent and summed in bfloat16 or wider, within the bound.
A program may use at most 64 MiB of HBM per device.

v0:
```python
import jax
import jax.numpy as jnp
from jax import lax
from jax.sharding import PartitionSpec as P

C = 70


def unit_vectors(polar, azimuth):
    sine_polar = jnp.sin(polar)
    return jnp.stack([sine_polar * jnp.cos(azimuth), sine_polar * jnp.sin(azimuth), jnp.cos(polar)])


def phase_tile(places, vectors):
    angles = (
        places[0][:, None] * vectors[0][None, :]
        + places[1][:, None] * vectors[1][None, :]
        + places[2][:, None] * vectors[2][None, :]
    )
    return (jnp.cos(angles).astype(jnp.bfloat16), jnp.sin(angles).astype(jnp.bfloat16))


def field_terms(coef_block, cos_tile, sin_tile):
    order_count = coef_block.shape[0] // 2
    real_rows = coef_block[:order_count]
    imag_rows = coef_block[order_count:]
    top_rows = jnp.concatenate([real_rows, imag_rows], axis=1)
    low_rows = jnp.concatenate([imag_rows, -real_rows], axis=1)
    left_side = jnp.concatenate([top_rows, low_rows], axis=0)
    right_side = jnp.concatenate([cos_tile, sin_tile], axis=0)
    return jnp.dot(left_side, right_side, preferred_element_type=jnp.float32)


def adjoint_terms(stacked, cos_tile, sin_tile):
    order_count = stacked.shape[0] // 2
    real_rows = stacked[:order_count]
    imag_rows = stacked[order_count:]
    top_rows = jnp.concatenate([real_rows, imag_rows], axis=1)
    low_rows = jnp.concatenate([imag_rows, -real_rows], axis=1)
    left_side = jnp.concatenate([top_rows, low_rows], axis=0)
    right_side = jnp.concatenate([cos_tile, sin_tile], axis=1)
    return lax.dot_general(
        left_side, right_side, (((1,), (1,)), ((), ())), preferred_element_type=jnp.float32
    )


def amplitude_parts(fields, farmap):
    order_count = fields.shape[0] // 2
    field_real = fields[:order_count][None]
    field_imag = fields[order_count:][None]
    map_real = farmap[:, 0]
    map_imag = farmap[:, 1]
    amp_real = jnp.sum(map_real * field_real - map_imag * field_imag, axis=1)
    amp_imag = jnp.sum(map_real * field_imag + map_imag * field_real, axis=1)
    return (amp_real, amp_imag)


def cotangent_from(amp_real, amp_imag, farmap, weights):
    map_real = farmap[:, 0]
    map_imag = farmap[:, 1]
    cot_real = weights * jnp.sum(
        amp_real[:, None] * map_real + amp_imag[:, None] * map_imag, axis=0
    )
    cot_imag = weights * jnp.sum(
        amp_real[:, None] * map_imag - amp_imag[:, None] * map_real, axis=0
    )
    return jnp.concatenate([cot_real, cot_imag], axis=0).astype(jnp.bfloat16)


def cotangent_rows(fields, farmap, weights):
    amp_real, amp_imag = amplitude_parts(fields, farmap)
    return cotangent_from(amp_real, amp_imag, farmap, weights)


def stacked_rows(adjoint, vectors):
    order_count = adjoint.shape[0] // 2
    widened = adjoint.astype(jnp.float32)
    scaled = [(vectors[axis_id][None, :] * widened).astype(jnp.bfloat16) for axis_id in range(3)]
    real_parts = [adjoint[:order_count]] + [item[:order_count] for item in scaled]
    imag_parts = [adjoint[order_count:]] + [item[order_count:] for item in scaled]
    return jnp.concatenate(real_parts + imag_parts, axis=0)


def gradients(output, coef_block):
    order_count = coef_block.shape[0] // 2
    real_out = output[: 4 * order_count]
    imag_out = output[4 * order_count :]
    coef_term = jnp.concatenate(
        [2.0 * real_out[:order_count], -2.0 * imag_out[:order_count]], axis=0
    )
    coef_real = coef_block[:order_count].astype(jnp.float32)
    coef_imag = coef_block[order_count:].astype(jnp.float32)
    place_terms = []
    for axis_id in range(3):
        lower_row = (axis_id + 1) * order_count
        upper_row = (axis_id + 2) * order_count
        place_terms.append(
            2.0
            * jnp.sum(
                coef_real * imag_out[lower_row:upper_row]
                + coef_imag * real_out[lower_row:upper_row],
                axis=0,
            )
        )
    return (coef_term, jnp.stack(place_terms))


def body(coefficients, positions, polar, azimuth, weights, farmap):
    own_count = coefficients.shape[2]
    own_rows = coefficients.reshape(2 * C, own_count)
    domain_rows = lax.all_gather(own_rows, "dir", axis=1, tiled=True)
    domain_places = lax.all_gather(positions, "dir", axis=1, tiled=True)
    vectors = unit_vectors(polar, azimuth)
    width_all = domain_rows.shape[1]
    width_block = 512
    blocks = width_all // width_block

    def forward_block(block_id, totals):
        offset = block_id * width_block
        coef_block = lax.dynamic_slice_in_dim(domain_rows, offset, width_block, 1)
        place_block = lax.dynamic_slice_in_dim(domain_places, offset, width_block, 1)
        cos_tile, sin_tile = phase_tile(place_block, vectors)
        return totals + field_terms(coef_block, cos_tile, sin_tile)

    partial_fields = lax.fori_loop(
        0, blocks, forward_block, jnp.zeros((2 * C, polar.shape[0]), jnp.float32)
    )
    fields = lax.psum(partial_fields, "dom")
    adjoint = cotangent_rows(fields, farmap, weights)
    stacked = stacked_rows(adjoint, vectors)

    def backward_block(block_id):
        offset = block_id * width_block
        coef_block = lax.dynamic_slice_in_dim(domain_rows, offset, width_block, 1)
        place_block = lax.dynamic_slice_in_dim(domain_places, offset, width_block, 1)
        cos_tile, sin_tile = phase_tile(place_block, vectors)
        return gradients(adjoint_terms(stacked, cos_tile, sin_tile), coef_block)

    coef_parts, place_parts = lax.map(backward_block, jnp.arange(blocks, dtype=jnp.int32))
    coef_part = jnp.moveaxis(coef_parts, 0, 1).reshape(2 * C, width_all)
    place_part = jnp.moveaxis(place_parts, 0, 1).reshape(3, width_all)
    coef_grad, place_grad = (
        lax.psum_scatter(coef_part, "dir", scatter_dimension=1, tiled=True),
        lax.psum_scatter(place_part, "dir", scatter_dimension=1, tiled=True),
    )
    return (coef_grad.reshape(2, C, own_count), place_grad)


def solution(mesh):
    placed = (
        P(None, None, ("dom", "dir")),
        P(None, ("dom", "dir")),
        P("dir"),
        P("dir"),
        P("dir"),
        P(None, None, None, "dir"),
    )
    return jax.shard_map(
        body,
        mesh=mesh,
        in_specs=placed,
        out_specs=(P(None, None, ("dom", "dir")), P(None, ("dom", "dir"))),
        check_vma=False,
    )
```

profile of v0, /device:TPU:8, one launch (start us, length us, event | category | flops | bytes accessed | tf_op | source)
XLA Modules:
  0.0 478.9 jit_solution(2724014570653692775)
XLA Ops:
  7.9 0.7 sine_multiply_fusion
  8.7 0.8 copy.18
  9.5 50.1 %all_gather.7 = bf16[140,2048]{1,0:T(8,128)(2,1)S(1)} all-gather(bf16[140,128]{1,0:T(8,128)(2,1)S(1)} %reshape.65), channel_id=1, replica_groups=mesh['dom'=16,'dir'=16] {'dir'}, dimensions={1}, use_global_device_ids=true | all-gather | bytes 609280 | tf_op jit(solution)/shard_map/all_gather | solution.py:111
  59.6 38.4 %all_gather.6 = f32[3,2048]{1,0:T(4,128)S(1)} all-gather(f32[3,128]{1,0:T(4,128)} %param.11), channel_id=1, replica_groups=mesh['dom'=16,'dir'=16] {'dir'}, dimensions={1}, use_global_device_ids=true | all-gather | bytes 26112 | tf_op jit(solution)/shard_map/all_gather | solution.py:112
  98.0 24.7 %while.29 = (s32[]{:T(128)}, f32[140,640]{1,0:T(8,128)S(1)}, bf16[140,2048]{1,0:T(8,128)(2,1)S(1)}, f32[3,2048]{1,0:T(4,128)S(1)}, f32[1,640]{1,0:T(1,128)S(1)},...) while((s32[]{:T(128)}, f32[140,640]{1,0:T(8,128)S(1)}, ...), condition=%wide.region_1.0_spmd.clone, body=%wide.region_0.0_spmd.clone.sunk | while | flops 189849616 | bytes 3953417 | solution.py:125
  98.2 5.4 %cosine_convert_fusion.5 = (bf16[512,640]{1,0:T(8,128)(2,1)S(1)}, bf16[512,640]{1,0:T(8,128)(2,1)S(1)}) fusion(f32[640]{0:T(1024)S(1)} %reduce.15, f32[512]{0:T(512)S(1)} %bitcast.83, f32[640]{0:T(1024)S(1)} %reduce.16, f32[512]{0:T(512)S(1)} %bitcast.82, f32[640]{0:T(1024)S(1)} %reduce.17, f32[512]{0:T(512)S(1)} %bitcast.81), kind=kLoop, calls=%fused_computation.35.clone.1 | loop fusion | flops 2293760 | bytes 1324544 | tf_op jit(solution)/shard_map/while/body/eval_jaxpr/convert_element_type | solution.py:20
  104.3 5.4 %cosine_convert_fusion.5 = (bf16[512,640]{1,0:T(8,128)(2,1)S(1)}, bf16[512,640]{1,0:T(8,128)(2,1)S(1)}) fusion(f32[640]{0:T(1024)S(1)} %reduce.15, f32[512]{0:T(512)S(1)} %bitcast.83, f32[640]{0:T(1024)S(1)} %reduce.16, f32[512]{0:T(512)S(1)} %bitcast.82, f32[640]{0:T(1024)S(1)} %reduce.17, f32[512]{0:T(512)S(1)} %bitcast.81), kind=kLoop, calls=%fused_computation.35.clone.1 | loop fusion | flops 2293760 | bytes 1324544 | tf_op jit(solution)/shard_map/while/body/eval_jaxpr/convert_element_type | solution.py:20
  110.5 5.4 %cosine_convert_fusion.5 = (bf16[512,640]{1,0:T(8,128)(2,1)S(1)}, bf16[512,640]{1,0:T(8,128)(2,1)S(1)}) fusion(f32[640]{0:T(1024)S(1)} %reduce.15, f32[512]{0:T(512)S(1)} %bitcast.83, f32[640]{0:T(1024)S(1)} %reduce.16, f32[512]{0:T(512)S(1)} %bitcast.82, f32[640]{0:T(1024)S(1)} %reduce.17, f32[512]{0:T(512)S(1)} %bitcast.81), kind=kLoop, calls=%fused_computation.35.clone.1 | loop fusion | flops 2293760 | bytes 1324544 | tf_op jit(solution)/shard_map/while/body/eval_jaxpr/convert_element_type | solution.py:20
  116.7 5.4 %cosine_convert_fusion.5 = (bf16[512,640]{1,0:T(8,128)(2,1)S(1)}, bf16[512,640]{1,0:T(8,128)(2,1)S(1)}) fusion(f32[640]{0:T(1024)S(1)} %reduce.15, f32[512]{0:T(512)S(1)} %bitcast.83, f32[640]{0:T(1024)S(1)} %reduce.16, f32[512]{0:T(512)S(1)} %bitcast.82, f32[640]{0:T(1024)S(1)} %reduce.17, f32[512]{0:T(512)S(1)} %bitcast.81), kind=kLoop, calls=%fused_computation.35.clone.1 | loop fusion | flops 2293760 | bytes 1324544 | tf_op jit(solution)/shard_map/while/body/eval_jaxpr/convert_element_type | solution.py:20
  124.3 113.6 %all-reduce.2.cloned.1.call-done = f32[140,640]{1,0:T(8,128)} async-done(((f32[140,640]{1,0:T(8,128)}), f32[140,640]{1,0:T(8,128)}) %all-reduce.2.cloned.1.call-update) | async-done | bytes 358416 | tf_op jit(solution)/shard_map/psum | solution.py:128
  237.9 1.0 fusion.32
  239.5 14.7 %maximum_maximum_fusion = bf16[560,1280]{1,0:T(8,128)(2,1)S(1)} fusion(bf16[280,640]{1,0:T(8,128)(2,1)S(1)} %maximum_negate_fusion, bf16[70,640]{1,0:T(8,128)(2,1)S(1)} %get-tuple-element.343, bf16[70,640]{1,0:T(8,128)(2,1)S(1)} %get-tuple-element.355, bf16[70,640]{1,0:T(8,128)(2,1)S(1)} %get-tuple-element.339, bf16[70,640]{1,0:T(8,128)(2,1)S(1)} %get-tuple-element.351, ...), kind=kLoop, calls=%fused_computation.48 | loop fusion | flops 18636800 | bytes 2508800 | tf_op jit(solution)/shard_map/while/body/eval_jaxpr/concatenate | solution.py:40
  254.2 35.1 %while.28 = (s32[]{:T(128)}, f32[4,140,512]{2,1,0:T(8,128)}, f32[4,3,512]{2,1,0:T(4,128)S(1)}, s32[4]{0:T(128)S(1)}, f32[3,2048]{1,0:T(4,128)S(1)}, /*index=5*/f...) while((s32[]{:T(128)}, f32[4,140,512]{2,1,0:T(8,128)}, ...), condition=%wide.region_11.12_spmd, body=%wide.region_7.11_spmd.sunk | while | flops 739566592 | bytes 7435559 | solution.py:139
  255.6 5.4 %cosine_convert_fusion.4 = (bf16[512,640]{1,0:T(8,128)(2,1)S(1)}, bf16[512,640]{1,0:T(8,128)(2,1)S(1)}) fusion(f32[640]{0:T(1024)S(1)} %reduce.12, f32[512]{0:T(512)S(1)} %bitcast.86, f32[640]{0:T(1024)S(1)} %reduce.13, f32[512]{0:T(512)S(1)} %bitcast.85, f32[640]{0:T(1024)S(1)} %reduce.14, f32[512]{0:T(512)S(1)} %bitcast.84), kind=kLoop, calls=%fused_computation.5.clone.1 | loop fusion | flops 2293760 | bytes 1324544 | tf_op jit(solution)/shard_map/while/body/eval_jaxpr/convert_element_type | solution.py:20
  261.1 0.9 convolution_bitcast_fusion.2
  262.3 0.7 fusion.50
  264.4 5.4 %cosine_convert_fusion.4 = (bf16[512,640]{1,0:T(8,128)(2,1)S(1)}, bf16[512,640]{1,0:T(8,128)(2,1)S(1)}) fusion(f32[640]{0:T(1024)S(1)} %reduce.12, f32[512]{0:T(512)S(1)} %bitcast.86, f32[640]{0:T(1024)S(1)} %reduce.13, f32[512]{0:T(512)S(1)} %bitcast.85, f32[640]{0:T(1024)S(1)} %reduce.14, f32[512]{0:T(512)S(1)} %bitcast.84), kind=kLoop, calls=%fused_computation.5.clone.1 | loop fusion | flops 2293760 | bytes 1324544 | tf_op jit(solution)/shard_map/while/body/eval_jaxpr/convert_element_type | solution.py:20
  269.9 0.9 convolution_bitcast_fusion.2
  271.1 0.7 fusion.50
  273.2 5.4 %cosine_convert_fusion.4 = (bf16[512,640]{1,0:T(8,128)(2,1)S(1)}, bf16[512,640]{1,0:T(8,128)(2,1)S(1)}) fusion(f32[640]{0:T(1024)S(1)} %reduce.12, f32[512]{0:T(512)S(1)} %bitcast.86, f32[640]{0:T(1024)S(1)} %reduce.13, f32[512]{0:T(512)S(1)} %bitcast.85, f32[640]{0:T(1024)S(1)} %reduce.14, f32[512]{0:T(512)S(1)} %bitcast.84), kind=kLoop, calls=%fused_computation.5.clone.1 | loop fusion | flops 2293760 | bytes 1324544 | tf_op jit(solution)/shard_map/while/body/eval_jaxpr/convert_element_type | solution.py:20
  278.6 0.9 convolution_bitcast_fusion.2
  279.9 0.7 fusion.50
  282.0 5.4 %cosine_convert_fusion.4 = (bf16[512,640]{1,0:T(8,128)(2,1)S(1)}, bf16[512,640]{1,0:T(8,128)(2,1)S(1)}) fusion(f32[640]{0:T(1024)S(1)} %reduce.12, f32[512]{0:T(512)S(1)} %bitcast.86, f32[640]{0:T(1024)S(1)} %reduce.13, f32[512]{0:T(512)S(1)} %bitcast.85, f32[640]{0:T(1024)S(1)} %reduce.14, f32[512]{0:T(512)S(1)} %bitcast.84), kind=kLoop, calls=%fused_computation.5.clone.1 | loop fusion | flops 2293760 | bytes 1324544 | tf_op jit(solution)/shard_map/while/body/eval_jaxpr/convert_element_type | solution.py:20
  287.4 0.9 convolution_bitcast_fusion.2
  288.6 0.7 fusion.50
  289.4 1.4 copy.23
  290.8 2.0 copy.20
  293.1 1.4 copy.27
  294.5 87.7 %reduce-scatter.7.cloned.1.call-done = f32[128,3]{1,0:T(8,128)} async-done(((f32[2048,3]{1,0:T(8,128)}), f32[128,3]{1,0:T(8,128)}) %reduce-scatter.7.cloned.1.call-update) | async-done | bytes 1552
  382.2 1.5 copy.24
  383.7 87.1 %reduce-scatter.5.cloned.1.call-done = f32[140,128]{1,0:T(8,128)} async-done(((f32[140,2048]{1,0:T(8,128)}), f32[140,128]{1,0:T(8,128)}) %reduce-scatter.5.cloned.1.call-update) | async-done | bytes 71696 | tf_op jit(solution)/shard_map/reduce_scatter | solution.py:143
  470.8 0.9 reshape.67
  (91 shorter events, 10.3 us)
Async XLA Ops:
  7.2 230.7 %all-reduce.2.cloned.1.call-start = ((), (), s32[]{:S(2)}) async-start(), calls=%async_computation.2 | async-start | bytes 737280 | tf_op jit(solution)/shard_map/psum | solution.py:128
  98.0 25.7 %copy-start = (f32[2,2,70,640]{3,1,2,0:T(2,128)S(1)}, f32[2,2,70,640]{3,1,2,0:T(2,128)}, u32[]{:S(2)}) copy-start(f32[2,2,70,640]{3,1,2,0:T(2,128)} %param.15) | copy-start | bytes 2150404
  122.7 0.7 copy-start.1
  123.4 258.8 %reduce-scatter.7.cloned.1.call-start = ((), (), s32[]{:S(2)}) async-start(), calls=%async_computation.4 | async-start | bytes 1114112
  124.3 114.9 %copy-start.2 = (f32[640]{0:T(1024)S(1)}, f32[640]{0:T(1024)}, u32[]{:S(2)}) copy-start(f32[640]{0:T(1024)} %param.14) | copy-start | bytes 7684
  290.8 180.0 %reduce-scatter.5.cloned.1.call-start = ((), (), s32[]{:S(2)}) async-start(), calls=%async_computation.3 | async-start | bytes 1253376 | tf_op jit(solution)/shard_map/reduce_scatter | solution.py:143
Sparse Core Ops, SparseCore 0:
  123.6 114.2 all-reduce.1
  290.9 91.2 reduce-scatter.6
  385.7 85.0 reduce-scatter.4
where the time goes:
time: 479 us
  waiting for transfers between devices  288 us (60%)
  blocking collectives  88.5 us (18%)
  other arithmetic  64.2 us (13%)
  local copies, waits for them, and re-layouts  15 us (3%)
  between operations  13.9 us (3%)
  matrix products  5.45 us (1%)
    psum x1, waiting for transfers between devices, body(): fields = lax.psum(partial_fields, 'dom')  114 us
    unnamed x4, waiting for transfers between devices  87.7 us
    reduce_scatter x1, waiting for transfers between devices, body(): lax.psum_scatter(coef_part, 'dir', scatter_dimension=1, tiled=True)  87.1 us
    all_gather x1, blocking collectives, body(): domain_rows = lax.all_gather(own_rows, 'dir', axis=1, tiled=True)  50.1 us
    convert_element_type x8, other arithmetic, phase_tile(): jnp.cos(angles).astype(jnp.bfloat16)  43.5 us
    all_gather x1, blocking collectives, body(): domain_places = lax.all_gather(positions, 'dir', axis=1, tiled=True)  38.4 us
    concatenate x1, other arithmetic, adjoint_terms(): left_side = jnp.concatenate([top_rows, low_rows], axis=0)  14.7 us
  transfers between devices with their start and end apart: 3, of which 3 were waited for; matrix products, arithmetic and copies ran while one was open for 1% of the time, Pallas kernels for 0%

commit v1 on v0

--- a/solution.py
+++ b/solution.py
@@ -108,7 +108,10 @@
 def body(coefficients, positions, polar, azimuth, weights, farmap):
     own_count = coefficients.shape[2]
     own_rows = coefficients.reshape(2 * C, own_count)
-    domain_rows = lax.all_gather(own_rows, "dir", axis=1, tiled=True)
+    size = lax.axis_size("dir")
+    tiles = jnp.stack([own_rows for _ in range(size)])
+    tiles = lax.all_to_all(tiles, "dir", split_axis=0, concat_axis=0)
+    domain_rows = jnp.concatenate(tiles, axis=1)
     domain_places = lax.all_gather(positions, "dir", axis=1, tiled=True)
     vectors = unit_vectors(polar, azimuth)
     width_all = domain_rows.shape[1]

time: 479 us -> 450 us (0.939)
  blocking collectives: 88.5 us -> 50.6 us
  starting transfers between devices: 0.3 us -> 11.3 us
    all_gather x1 -> x0, blocking collectives: 50.1 us -> none  [body(): domain_rows = lax.all_gather(own_rows, 'dir', axis=1, tiled=True)]
    all_gather x1, blocking collectives: 38.4 us -> 50.6 us  [body(): domain_places = lax.all_gather(positions, 'dir', axis=1, tiled=True)]
    all_to_all x0 -> x1, starting transfers between devices: none -> 11 us  [body(): tiles = lax.all_to_all(tiles, 'dir', split_axis=0, concat_axis=0)]
  transfers between devices with their start and end apart: 3 -> 4, of which waited for: 3 -> 3; matrix products, arithmetic and copies ran while one was open for 1% -> 1% of each run, Pallas kernels for 0% -> 0%
where the time goes in v1:
time: 450 us
  waiting for transfers between devices  286 us (64%)
  other arithmetic  63.5 us (14%)
  blocking collectives  50.6 us (11%)
  local copies, waits for them, and re-layouts  15.7 us (3%)
  between operations  14 us (3%)
  starting transfers between devices  11.3 us (3%)
  matrix products  5.45 us (1%)
    psum x1, waiting for transfers between devices, body(): fields = lax.psum(partial_fields, 'dom')  111 us
    unnamed x4, waiting for transfers between devices  87.9 us
    reduce_scatter x1, waiting for transfers between devices, body(): lax.psum_scatter(coef_part, 'dir', scatter_dimension=1, tiled=True)  87.1 us
    all_gather x1, blocking collectives, body(): domain_places = lax.all_gather(positions, 'dir', axis=1, tiled=True)  50.6 us
    convert_element_type x8, other arithmetic, phase_tile(): jnp.cos(angles).astype(jnp.bfloat16)  43.6 us
    concatenate x1, other arithmetic, adjoint_terms(): left_side = jnp.concatenate([top_rows, low_rows], axis=0)  14.7 us
    all_to_all x1, starting transfers between devices, body(): tiles = lax.all_to_all(tiles, 'dir', split_axis=0, concat_axis=0)  11 us
  transfers between devices with their start and end apart: 4, of which 3 were waited for; matrix products, arithmetic and copies ran while one was open for 1% of the time, Pallas kernels for 0%

profile of v1, /device:TPU:8, one launch (start us, length us, event | category | flops | bytes accessed | tf_op | source)
XLA Modules:
  0.0 449.8 jit_solution(11085063543772548002)
XLA Ops:
  7.2 0.8 copy.23
  8.0 0.9 stack.23
  8.9 11.0 %all-to-all-start = ((bf16[16,140,128]{2,1,0:T(8,128)(2,1)}), bf16[16,140,128]{2,1,0:T(8,128)(2,1)S(1)}, u32[]{:S(2)}, u32[]{:S(2)}) async-start(bf16[16,140,128]{2,1,0:T(8,128)(2,1)} %stack.23), calls=%async_computation | async-start | bytes 1179648 | tf_op jit(solution)/shard_map/all_to_all | solution.py:113
  20.1 50.6 %all_gather.3 = f32[3,2048]{1,0:T(4,128)S(1)} all-gather(f32[3,128]{1,0:T(4,128)S(1)} %copy-done.5), channel_id=1, replica_groups=mesh['dom'=16,'dir'=16] {'dir'}, dimensions={1}, use_global_device_ids=true | all-gather | bytes 26112 | tf_op jit(solution)/shard_map/all_gather | solution.py:115
  71.2 24.7 %while.29 = (s32[]{:T(128)}, f32[140,640]{1,0:T(8,128)S(1)}, bf16[140,2048]{1,0:T(8,128)(2,1)S(1)}, f32[3,2048]{1,0:T(4,128)S(1)}, f32[1,640]{1,0:T(1,128)S(1)},...) while((s32[]{:T(128)}, f32[140,640]{1,0:T(8,128)S(1)}, ...), condition=%wide.region_1.0_spmd.clone, body=%wide.region_0.0_spmd.clone.sunk | while | flops 189849616 | bytes 3953417 | solution.py:128
  71.3 5.4 %cosine_convert_fusion.5 = (bf16[512,640]{1,0:T(8,128)(2,1)S(1)}, bf16[512,640]{1,0:T(8,128)(2,1)S(1)}) fusion(f32[640]{0:T(1024)S(1)} %reduce.15, f32[512]{0:T(512)S(1)} %bitcast.90, f32[640]{0:T(1024)S(1)} %reduce.16, f32[512]{0:T(512)S(1)} %bitcast.89, f32[640]{0:T(1024)S(1)} %reduce.17, f32[512]{0:T(512)S(1)} %bitcast.88), kind=kLoop, calls=%fused_computation.35.clone.1 | loop fusion | flops 2293760 | bytes 1324544 | tf_op jit(solution)/shard_map/while/body/eval_jaxpr/convert_element_type | solution.py:20
  77.5 5.4 %cosine_convert_fusion.5 = (bf16[512,640]{1,0:T(8,128)(2,1)S(1)}, bf16[512,640]{1,0:T(8,128)(2,1)S(1)}) fusion(f32[640]{0:T(1024)S(1)} %reduce.15, f32[512]{0:T(512)S(1)} %bitcast.90, f32[640]{0:T(1024)S(1)} %reduce.16, f32[512]{0:T(512)S(1)} %bitcast.89, f32[640]{0:T(1024)S(1)} %reduce.17, f32[512]{0:T(512)S(1)} %bitcast.88), kind=kLoop, calls=%fused_computation.35.clone.1 | loop fusion | flops 2293760 | bytes 1324544 | tf_op jit(solution)/shard_map/while/body/eval_jaxpr/convert_element_type | solution.py:20
  83.7 5.4 %cosine_convert_fusion.5 = (bf16[512,640]{1,0:T(8,128)(2,1)S(1)}, bf16[512,640]{1,0:T(8,128)(2,1)S(1)}) fusion(f32[640]{0:T(1024)S(1)} %reduce.15, f32[512]{0:T(512)S(1)} %bitcast.90, f32[640]{0:T(1024)S(1)} %reduce.16, f32[512]{0:T(512)S(1)} %bitcast.89, f32[640]{0:T(1024)S(1)} %reduce.17, f32[512]{0:T(512)S(1)} %bitcast.88), kind=kLoop, calls=%fused_computation.35.clone.1 | loop fusion | flops 2293760 | bytes 1324544 | tf_op jit(solution)/shard_map/while/body/eval_jaxpr/convert_element_type | solution.py:20
  89.8 5.4 %cosine_convert_fusion.5 = (bf16[512,640]{1,0:T(8,128)(2,1)S(1)}, bf16[512,640]{1,0:T(8,128)(2,1)S(1)}) fusion(f32[640]{0:T(1024)S(1)} %reduce.15, f32[512]{0:T(512)S(1)} %bitcast.90, f32[640]{0:T(1024)S(1)} %reduce.16, f32[512]{0:T(512)S(1)} %bitcast.89, f32[640]{0:T(1024)S(1)} %reduce.17, f32[512]{0:T(512)S(1)} %bitcast.88), kind=kLoop, calls=%fused_computation.35.clone.1 | loop fusion | flops 2293760 | bytes 1324544 | tf_op jit(solution)/shard_map/while/body/eval_jaxpr/convert_element_type | solution.py:20
  97.5 111.1 %all-reduce.2.cloned.1.call-done = f32[140,640]{1,0:T(8,128)} async-done(((f32[140,640]{1,0:T(8,128)}), f32[140,640]{1,0:T(8,128)}) %all-reduce.2.cloned.1.call-update) | async-done | bytes 358416 | tf_op jit(solution)/shard_map/psum | solution.py:131
  208.6 1.0 fusion.32
  210.2 14.7 %maximum_maximum_fusion = bf16[560,1280]{1,0:T(8,128)(2,1)S(1)} fusion(bf16[280,640]{1,0:T(8,128)(2,1)S(1)} %maximum_negate_fusion, bf16[70,640]{1,0:T(8,128)(2,1)S(1)} %get-tuple-element.345, bf16[70,640]{1,0:T(8,128)(2,1)S(1)} %get-tuple-element.357, bf16[70,640]{1,0:T(8,128)(2,1)S(1)} %get-tuple-element.341, bf16[70,640]{1,0:T(8,128)(2,1)S(1)} %get-tuple-element.353, ...), kind=kLoop, calls=%fused_computation.48 | loop fusion | flops 18636800 | bytes 2508800 | tf_op jit(solution)/shard_map/while/body/eval_jaxpr/concatenate | solution.py:40
  224.9 35.2 %while.28 = (s32[]{:T(128)}, f32[4,140,512]{2,1,0:T(8,128)}, f32[4,3,512]{2,1,0:T(4,128)S(1)}, s32[4]{0:T(128)S(1)}, f32[3,2048]{1,0:T(4,128)S(1)}, /*index=5*/f...) while((s32[]{:T(128)}, f32[4,140,512]{2,1,0:T(8,128)}, ...), condition=%wide.region_11.12_spmd, body=%wide.region_7.11_spmd.sunk | while | flops 739566592 | bytes 7435559 | solution.py:142
  226.3 5.5 %cosine_convert_fusion.4 = (bf16[512,640]{1,0:T(8,128)(2,1)S(1)}, bf16[512,640]{1,0:T(8,128)(2,1)S(1)}) fusion(f32[640]{0:T(1024)S(1)} %reduce.12, f32[512]{0:T(512)S(1)} %bitcast.93, f32[640]{0:T(1024)S(1)} %reduce.13, f32[512]{0:T(512)S(1)} %bitcast.92, f32[640]{0:T(1024)S(1)} %reduce.14, f32[512]{0:T(512)S(1)} %bitcast.91), kind=kLoop, calls=%fused_computation.5.clone.1 | loop fusion | flops 2293760 | bytes 1324544 | tf_op jit(solution)/shard_map/while/body/eval_jaxpr/convert_element_type | solution.py:20
  231.8 0.9 convolution_bitcast_fusion.2
  233.0 0.7 fusion.50
  235.1 5.5 %cosine_convert_fusion.4 = (bf16[512,640]{1,0:T(8,128)(2,1)S(1)}, bf16[512,640]{1,0:T(8,128)(2,1)S(1)}) fusion(f32[640]{0:T(1024)S(1)} %reduce.12, f32[512]{0:T(512)S(1)} %bitcast.93, f32[640]{0:T(1024)S(1)} %reduce.13, f32[512]{0:T(512)S(1)} %bitcast.92, f32[640]{0:T(1024)S(1)} %reduce.14, f32[512]{0:T(512)S(1)} %bitcast.91), kind=kLoop, calls=%fused_computation.5.clone.1 | loop fusion | flops 2293760 | bytes 1324544 | tf_op jit(solution)/shard_map/while/body/eval_jaxpr/convert_element_type | solution.py:20
  240.6 0.9 convolution_bitcast_fusion.2
  241.8 0.7 fusion.50
  243.9 5.5 %cosine_convert_fusion.4 = (bf16[512,640]{1,0:T(8,128)(2,1)S(1)}, bf16[512,640]{1,0:T(8,128)(2,1)S(1)}) fusion(f32[640]{0:T(1024)S(1)} %reduce.12, f32[512]{0:T(512)S(1)} %bitcast.93, f32[640]{0:T(1024)S(1)} %reduce.13, f32[512]{0:T(512)S(1)} %bitcast.92, f32[640]{0:T(1024)S(1)} %reduce.14, f32[512]{0:T(512)S(1)} %bitcast.91), kind=kLoop, calls=%fused_computation.5.clone.1 | loop fusion | flops 2293760 | bytes 1324544 | tf_op jit(solution)/shard_map/while/body/eval_jaxpr/convert_element_type | solution.py:20
  249.4 0.9 convolution_bitcast_fusion.2
  250.6 0.7 fusion.50
  252.7 5.5 %cosine_convert_fusion.4 = (bf16[512,640]{1,0:T(8,128)(2,1)S(1)}, bf16[512,640]{1,0:T(8,128)(2,1)S(1)}) fusion(f32[640]{0:T(1024)S(1)} %reduce.12, f32[512]{0:T(512)S(1)} %bitcast.93, f32[640]{0:T(1024)S(1)} %reduce.13, f32[512]{0:T(512)S(1)} %bitcast.92, f32[640]{0:T(1024)S(1)} %reduce.14, f32[512]{0:T(512)S(1)} %bitcast.91), kind=kLoop, calls=%fused_computation.5.clone.1 | loop fusion | flops 2293760 | bytes 1324544 | tf_op jit(solution)/shard_map/while/body/eval_jaxpr/convert_element_type | solution.py:20
  258.2 0.9 convolution_bitcast_fusion.2
  259.4 0.7 fusion.50
  260.1 1.4 copy.29
  261.6 2.0 copy.26
  263.8 1.4 copy.34
  265.3 87.9 %reduce-scatter.7.cloned.1.call-done = f32[128,3]{1,0:T(8,128)} async-done(((f32[2048,3]{1,0:T(8,128)}), f32[128,3]{1,0:T(8,128)}) %reduce-scatter.7.cloned.1.call-update) | async-done | bytes 1552
  353.1 1.5 copy.30
  354.6 87.1 %reduce-scatter.5.cloned.1.call-done = f32[140,128]{1,0:T(8,128)} async-done(((f32[140,2048]{1,0:T(8,128)}), f32[140,128]{1,0:T(8,128)}) %reduce-scatter.5.cloned.1.call-update) | async-done | bytes 71696 | tf_op jit(solution)/shard_map/reduce_scatter | solution.py:146
  441.7 0.9 reshape.73
  (102 shorter events, 10.1 us)
Async XLA Ops:
  7.2 12.8 %copy-start.3 = (f32[640]{0:T(1024)S(1)}, f32[640]{0:T(1024)}, u32[]{:S(2)}) copy-start(f32[640]{0:T(1024)} %param.12) | copy-start | bytes 7684
  7.2 12.9 %copy-start.4 = (f32[640]{0:T(1024)S(1)}, f32[640]{0:T(1024)}, u32[]{:S(2)}) copy-start(f32[640]{0:T(1024)} %param.13) | copy-start | bytes 7684
  7.2 12.9 %copy-start.5 = (f32[3,128]{1,0:T(4,128)S(1)}, f32[3,128]{1,0:T(4,128)}, u32[]{:S(2)}) copy-start(f32[3,128]{1,0:T(4,128)} %param.11) | copy-start | bytes 4612
  8.9 61.8 %all-to-all-start = ((bf16[16,140,128]{2,1,0:T(8,128)(2,1)}), bf16[16,140,128]{2,1,0:T(8,128)(2,1)S(1)}, u32[]{:S(2)}, u32[]{:S(2)}) async-start(bf16[16,140,128]{2,1,0:T(8,128)(2,1)} %stack.23), calls=%async_computation | async-start | bytes 1179648 | tf_op jit(solution)/shard_map/all_to_all | solution.py:113
  19.9 188.6 %all-reduce.2.cloned.1.call-start = ((), (), s32[]{:S(2)}) async-start(), calls=%async_computation.3 | async-start | bytes 737280 | tf_op jit(solution)/shard_map/psum | solution.py:131
  71.2 25.7 %copy-start = (f32[2,2,70,640]{3,1,2,0:T(2,128)S(1)}, f32[2,2,70,640]{3,1,2,0:T(2,128)}, u32[]{:S(2)}) copy-start(f32[2,2,70,640]{3,1,2,0:T(2,128)} %param.15) | copy-start | bytes 2150404
  95.9 0.7 copy-start.1
  96.6 256.5 %reduce-scatter.7.cloned.1.call-start = ((), (), s32[]{:S(2)}) async-start(), calls=%async_computation.5 | async-start | bytes 1114112
  97.4 112.4 %copy-start.2 = (f32[640]{0:T(1024)S(1)}, f32[640]{0:T(1024)}, u32[]{:S(2)}) copy-start(f32[640]{0:T(1024)} %param.14) | copy-start | bytes 7684
  261.6 180.2 %reduce-scatter.5.cloned.1.call-start = ((), (), s32[]{:S(2)}) async-start(), calls=%async_computation.4 | async-start | bytes 1253376 | tf_op jit(solution)/shard_map/reduce_scatter | solution.py:146
Sparse Core Ops, SparseCore 0:
  96.7 111.7 all-reduce.1
  261.7 91.3 reduce-scatter.6
  356.6 85.0 reduce-scatter.4
